TPU v7x, 256 devices: a whole 4x4x8 slice. The times are simulated.
256 devices in a mesh: au: 32 (over y, x, core), ia: 8 (over z).
Axes of the slice: x: 4, y: 4, z: 8, core: 2. Of those that a mesh axis runs over, the one named last changes fastest.
Arguments:
- user_emb: float32 [131072, 128], P(('au', 'ia')), may hold values from -6 to 6
- item_emb: float32 [32768, 128], P(('ia', 'au')), may hold values from -6 to 6
- user_degree: int32 [131072], P(('au', 'ia')), may hold values from 1 to 64
- item_degree: int32 [32768], P(('ia', 'au')), may hold values from 1 to 64
- tiles: float32 [32768, 128, 128], P(('au', 'ia')), as said below
- tile_user_block: int32 [32768], P(('au', 'ia')), may hold values from 0 to 31
- tile_item_block: int32 [32768], P(('au', 'ia')), may hold values from 0 to 31
- live_tiles: int32 [256], P(('au', 'ia')), may hold values from 32 to 128, as said below
Outputs:
- user_final: float32 [131072, 128], P(('au', 'ia'))
- item_final: float32 [32768, 128], P(('ia', 'au'))
Inputs may be any that keep to these rules, and one draw needn't show every extreme that they name: Tile slots of grid cell c beyond the first live_tiles[c] are unused; some cell uses all 128. `tiles`: each tile holds weights of 0 or between 0.05 and 0.35.
All inputs are finite; a program needn't handle non-finite values.
Results may differ from a plain program's by a relative error of at most 0.0001.
Values sent between devices are 32-bit elements; how exact they have to be, the bound alone decides.
A program may use at most 128 MiB of HBM per device.

v0:
```python
import jax
import jax.numpy as jnp
from jax import lax
from jax.sharding import PartitionSpec as P

LAYERS = 2


def per_device(
    user_emb,
    item_emb,
    user_degree,
    item_degree,
    tiles,
    tile_user_block,
    tile_item_block,
    live_tiles,
):
    tile_size = tiles.shape[1]
    emb_width = user_emb.shape[1]
    tile_count = tiles.shape[0]
    user_count = user_emb.shape[0]
    user_blocks = user_count * lax.axis_size("ia") // tile_size
    item_blocks = item_emb.shape[0] * lax.axis_size("au") // tile_size
    live_mask = (jnp.arange(tile_count, dtype=jnp.int32) < live_tiles[0]).astype(jnp.float32)
    user_pick = (
        tile_user_block[None, :] == jnp.arange(user_blocks, dtype=jnp.int32)[:, None]
    ).astype(jnp.float32) * live_mask[None, :]
    item_pick = (
        tile_item_block[None, :] == jnp.arange(item_blocks, dtype=jnp.int32)[:, None]
    ).astype(jnp.float32) * live_mask[None, :]
    norm_user = lax.rsqrt(user_degree.astype(jnp.float32))[:, None]
    norm_item = lax.rsqrt(item_degree.astype(jnp.float32))[:, None]
    gathered_users = lax.all_gather(user_emb * norm_user, "ia", axis=0, tiled=True)
    users_now, items_now = (user_emb, item_emb)
    user_total, item_total = (user_emb, item_emb)
    for layer_index in range(LAYERS):
        gathered_items = lax.all_gather(items_now * norm_item, "au", axis=0, tiled=True)
        toward_picked = gathered_items.reshape(item_blocks, tile_size, emb_width)[tile_item_block]
        toward_products = jnp.einsum(
            "tuk,tkd->tud", tiles, toward_picked, precision=lax.Precision.HIGHEST
        )
        toward_summed = jnp.dot(
            user_pick, toward_products.reshape(tile_count, -1), precision=lax.Precision.HIGHEST
        )
        partial_users = toward_summed.reshape(user_blocks * tile_size, emb_width)
        picked = gathered_users.reshape(user_blocks, tile_size, emb_width)[tile_user_block]
        products = jnp.einsum("tuk,tud->tkd", tiles, picked, precision=lax.Precision.HIGHEST)
        summed = jnp.dot(
            item_pick, products.reshape(tile_count, -1), precision=lax.Precision.HIGHEST
        )
        partial_items = summed.reshape(item_blocks * tile_size, emb_width)
        users_now = (
            lax.psum_scatter(partial_users, "ia", scatter_dimension=0, tiled=True) * norm_user
        )
        if layer_index + 1 < LAYERS:
            gathered_users = lax.all_gather(users_now * norm_user, "ia", axis=0, tiled=True)
        items_now = (
            lax.psum_scatter(partial_items, "au", scatter_dimension=0, tiled=True) * norm_item
        )
        user_total = user_total + users_now
        item_total = item_total + items_now
    return (user_total / (LAYERS + 1.0), item_total / (LAYERS + 1.0))


def solution(mesh):
    in_specs = (
        P(("au", "ia"), None),
        P(("ia", "au"), None),
        P(("au", "ia")),
        P(("ia", "au")),
        P(("au", "ia"), None, None),
        P(("au", "ia")),
        P(("au", "ia")),
        P(("au", "ia")),
    )
    out_specs = (P(("au", "ia"), None), P(("ia", "au"), None))
    return jax.shard_map(
        per_device, mesh=mesh, in_specs=in_specs, out_specs=out_specs, check_vma=False
    )
```

profile of v0, /device:TPU:2, one launch (start us, length us, event | category | flops | bytes accessed | tf_op | source)
XLA Modules:
  0.0 559.2 jit_solution(12804511916847766787)
XLA Ops:
  7.2 0.0 all-gather.7.cloned.1.call-start
  7.2 0.7 convert_rsqrt_fusion
  7.9 1.8 broadcast_multiply_fusion
  9.7 0.0 all-gather.7.cloned.1.call-update
  9.7 0.0 reduce-scatter.7.cloned.1.call-start
  10.4 0.7 compare_select_fusion
  11.1 43.4 %all-gather.7.cloned.1.call-done = f32[4096,128]{1,0:T(8,128)} async-done(((f32[512,128]{1,0:T(8,128)}), f32[4096,128]{1,0:T(8,128)}) %all-gather.7.cloned.1.call-update) | async-done | bytes 2097168 | tf_op jit(solution)/shard_map/all_gather | solution.py:34
  54.5 5.9 %gather_fusion.1 = f32[128,128,128]{2,1,0:T(8,128)} fusion(f32[32,128,128]{2,1,0:T(8,128)} %bitcast.32, s32[1024]{0:T(1024)S(1)} %pad_clamp_fusion), kind=kCustom, calls=%fused_computation.1 | custom fusion | bytes 16777728 | tf_op jit(solution)/shard_map/gather | solution.py:47
  60.4 19.0 %convolution_bitcast_fusion.2 = f32[128,128,128]{1,2,0:T(8,128)} fusion(f32[128,128,128]{2,1,0:T(8,128)} %gather_fusion.1, f32[128,128,128]{2,1,0:T(8,128)} %param.12), kind=kOutput, calls=%fused_computation.6 | convolution fusion | flops 3221225472 | bytes 25165824 | tf_op jit(solution)/shard_map/tuk,tud->tkd/dot_general | solution.py:48
  79.4 9.4 %copy.13 = f32[128,128,128]{0,2,1:T(8,128)} copy(f32[128,128,128]{1,2,0:T(8,128)} %convolution_bitcast_fusion.2) | data formatting | bytes 16777216 | tf_op jit(solution)/shard_map/tuk,tud->tkd/dot_general | solution.py:48
  88.8 10.8 %fusion.2 = f32[32,16384]{1,0:T(8,128)S(1)} fusion(f32[128,16384]{0,1:T(8,128)} %bitcast.35, s32[128]{0:T(128)S(1)} %copy-done.4, f32[128]{0:T(128)S(1)} %compare_convert_fusion), kind=kOutput, calls=%fused_computation.16 | convolution fusion | flops 805314560 | bytes 10486784 | tf_op jit(solution)/shard_map/dot_general | solution.py:49
  99.6 1.5 reshape.54
  101.1 0.0 reduce-scatter.7.cloned.1.call-update
  101.1 0.0 all-gather.9.cloned.1.call-start
  101.2 84.7 %reduce-scatter.7.cloned.1.call-done = f32[128,128]{1,0:T(8,128)} async-done(((f32[4096,128]{1,0:T(8,128)}), f32[128,128]{1,0:T(8,128)}) %reduce-scatter.7.cloned.1.call-update) | async-done | bytes 65552 | tf_op jit(solution)/shard_map/reduce_scatter | solution.py:59
  185.9 1.6 broadcast_multiply_fusion.1
  187.5 0.0 all-gather.9.cloned.1.call-update
  187.5 0.0 all-gather.5.cloned.1.call-start
  187.6 0.5 all-gather.5.cloned.1.call-update
  188.1 0.5 reduce-scatter.9.cloned.1.call-start
  188.6 48.6 %all-gather.9.cloned.1.call-done = f32[4096,128]{1,0:T(8,128)} async-done(((f32[128,128]{1,0:T(8,128)}), f32[4096,128]{1,0:T(8,128)}) %all-gather.9.cloned.1.call-update) | async-done | bytes 2097168 | tf_op jit(solution)/shard_map/all_gather | solution.py:38
  237.2 5.9 %gather_fusion.2 = f32[128,128,128]{2,1,0:T(8,128)} fusion(f32[32,128,128]{2,1,0:T(8,128)} %bitcast.31, s32[1024]{0:T(1024)S(1)} %pad_clamp_fusion.1), kind=kCustom, calls=%fused_computation.2 | custom fusion | bytes 16777728 | tf_op jit(solution)/shard_map/gather | solution.py:39
  243.1 19.0 %convolution_bitcast_fusion.1 = f32[128,128,128]{1,2,0:T(8,128)} fusion(f32[128,128,128]{2,1,0:T(8,128)} %gather_fusion.2, f32[128,128,128]{2,1,0:T(8,128)} %param.12), kind=kOutput, calls=%fused_computation.5 | convolution fusion | flops 3221225472 | bytes 25165824 | tf_op jit(solution)/shard_map/tuk,tkd->tud/dot_general | solution.py:40
  262.1 9.4 %copy.15 = f32[128,128,128]{0,2,1:T(8,128)} copy(f32[128,128,128]{1,2,0:T(8,128)} %convolution_bitcast_fusion.1) | data formatting | bytes 16777216 | tf_op jit(solution)/shard_map/tuk,tkd->tud/dot_general | solution.py:40
  271.6 10.7 %fusion.4 = f32[32,16384]{1,0:T(8,128)S(1)} fusion(f32[128,16384]{0,1:T(8,128)} %bitcast.36, f32[128]{0:T(128)S(1)} %compare_convert_fusion, s32[128]{0:T(128)S(1)} %copy-done.3), kind=kOutput, calls=%fused_computation.18 | convolution fusion | flops 805314560 | bytes 10486784 | tf_op jit(solution)/shard_map/dot_general | solution.py:43
  282.3 1.5 reshape.57
  283.8 0.0 reduce-scatter.9.cloned.1.call-update
  283.8 0.2 reduce-scatter.5.cloned.1.call-start
  284.1 4.3 all-gather.5.cloned.1.call-done
  288.4 5.9 %gather_fusion = f32[128,128,128]{2,1,0:T(8,128)} fusion(f32[32,128,128]{2,1,0:T(8,128)} %bitcast.30, s32[1024]{0:T(1024)S(1)} %pad_clamp_fusion.1), kind=kCustom, calls=%fused_computation | custom fusion | bytes 16777728 | tf_op jit(solution)/shard_map/gather | solution.py:39
  294.3 19.0 %convolution_bitcast_fusion.3 = f32[128,128,128]{1,2,0:T(8,128)} fusion(f32[128,128,128]{2,1,0:T(8,128)} %gather_fusion, f32[128,128,128]{2,1,0:T(8,128)} %param.12), kind=kOutput, calls=%fused_computation.7 | convolution fusion | flops 3221225472 | bytes 25165824 | tf_op jit(solution)/shard_map/tuk,tkd->tud/dot_general | solution.py:40
  313.3 9.5 %copy.11 = f32[128,128,128]{0,2,1:T(8,128)} copy(f32[128,128,128]{1,2,0:T(8,128)} %convolution_bitcast_fusion.3) | data formatting | bytes 16777216 | tf_op jit(solution)/shard_map/tuk,tkd->tud/dot_general | solution.py:40
  322.7 10.8 %fusion.6 = f32[32,16384]{1,0:T(8,128)S(1)} fusion(f32[128,16384]{0,1:T(8,128)} %bitcast.37, f32[128]{0:T(128)S(1)} %compare_convert_fusion, s32[128]{0:T(128)S(1)} %copy-done.3), kind=kOutput, calls=%fused_computation.20 | convolution fusion | flops 805314560 | bytes 10486784 | tf_op jit(solution)/shard_map/dot_general | solution.py:43
  333.5 1.5 reshape.51
  335.1 0.0 all-gather.11.cloned.1.call-start
  335.1 0.0 reduce-scatter.9.cloned.1.call-done
  335.2 41.9 %reduce-scatter.5.cloned.1.call-done = f32[512,128]{1,0:T(8,128)} async-done(((f32[4096,128]{1,0:T(8,128)}), f32[512,128]{1,0:T(8,128)}) %reduce-scatter.5.cloned.1.call-update) | async-done | bytes 262160 | tf_op jit(solution)/shard_map/reduce_scatter | solution.py:54
  377.1 2.0 multiply_multiply_fusion
  379.0 0.0 all-gather.11.cloned.1.call-update
  379.1 0.3 reduce-scatter.11.cloned.1.call-start
  379.3 39.8 %all-gather.11.cloned.1.call-done = f32[4096,128]{1,0:T(8,128)} async-done(((f32[512,128]{1,0:T(8,128)}), f32[4096,128]{1,0:T(8,128)}) %all-gather.11.cloned.1.call-update) | async-done | bytes 2097168 | tf_op jit(solution)/shard_map/all_gather | solution.py:57
  419.2 5.9 %gather_fusion.3 = f32[128,128,128]{2,1,0:T(8,128)} fusion(f32[32,128,128]{2,1,0:T(8,128)} %bitcast.33, s32[1024]{0:T(1024)S(1)} %pad_clamp_fusion), kind=kCustom, calls=%fused_computation.3 | custom fusion | bytes 16777728 | tf_op jit(solution)/shard_map/gather | solution.py:47
  425.1 19.0 %convolution_bitcast_fusion = f32[128,128,128]{1,2,0:T(8,128)} fusion(f32[128,128,128]{2,1,0:T(8,128)} %gather_fusion.3, f32[128,128,128]{2,1,0:T(8,128)} %param.12), kind=kOutput, calls=%fused_computation.4 | convolution fusion | flops 3221225472 | bytes 25165824 | tf_op jit(solution)/shard_map/tuk,tud->tkd/dot_general | solution.py:48
  444.1 9.4 %copy.17 = f32[128,128,128]{0,2,1:T(8,128)} copy(f32[128,128,128]{1,2,0:T(8,128)} %convolution_bitcast_fusion) | data formatting | bytes 16777216 | tf_op jit(solution)/shard_map/tuk,tud->tkd/dot_general | solution.py:48
  453.5 10.7 %fusion = f32[32,16384]{1,0:T(8,128)S(1)} fusion(f32[128,16384]{0,1:T(8,128)} %bitcast.34, s32[128]{0:T(128)S(1)} %copy-done.4, f32[128]{0:T(128)S(1)} %compare_convert_fusion), kind=kOutput, calls=%fused_computation.14 | convolution fusion | flops 805314560 | bytes 10486784 | tf_op jit(solution)/shard_map/dot_general | solution.py:49
  464.3 1.5 reshape.60
  465.8 84.8 %reduce-scatter.11.cloned.1.call-done = f32[128,128]{1,0:T(8,128)} async-done(((f32[4096,128]{1,0:T(8,128)}), f32[128,128]{1,0:T(8,128)}) %reduce-scatter.11.cloned.1.call-update) | async-done | bytes 65552 | tf_op jit(solution)/shard_map/reduce_scatter | solution.py:59
  550.6 1.6 add_multiply_fusion.1
  (19 shorter events, 0.1 us)
Async XLA Ops:
  7.2 47.3 %all-gather.7.cloned.1.call-start = ((), (), s32[]{:S(2)}) async-start(), calls=%async_computation.6 | async-start | bytes 2359296 | tf_op jit(solution)/shard_map/all_gather | solution.py:34
  9.7 176.2 %reduce-scatter.7.cloned.1.call-start = ((), (), s32[]{:S(2)}) async-start(), calls=%async_computation.7 | async-start | bytes 2162688 | tf_op jit(solution)/shard_map/reduce_scatter | solution.py:59
  79.4 9.4 %copy-start.4 = (s32[128]{0:T(128)S(1)}, s32[128]{0:T(128)}, u32[]{:S(2)}) copy-start(s32[128]{0:T(128)} %param.14) | copy-start | bytes 1540
  88.8 12.4 %copy-start.5 = (s32[128]{0:T(128)S(1)}, s32[128]{0:T(128)}, u32[]{:S(2)}) copy-start(s32[128]{0:T(128)} %param.11) | copy-start | bytes 1540
  88.8 97.1 %copy-start.1 = (f32[128,128]{1,0:T(8,128)S(1)}, f32[128,128]{1,0:T(8,128)}, u32[]{:S(2)}) copy-start(f32[128,128]{1,0:T(8,128)} %param.9) | copy-start | bytes 196612
  101.1 136.1 %all-gather.9.cloned.1.call-start = ((), (), s32[]{:S(2)}) async-start(), calls=%async_computation.8 | async-start | bytes 2162688 | tf_op jit(solution)/shard_map/all_gather | solution.py:38
  187.5 100.9 %all-gather.5.cloned.1.call-start = ((), (), s32[]{:S(2)}) async-start(), calls=%async_computation.4 | async-start | bytes 2162688 | tf_op jit(solution)/shard_map/all_gather | solution.py:38
  188.1 147.1 %reduce-scatter.9.cloned.1.call-start = ((), (), s32[]{:S(2)}) async-start(), calls=%async_computation.9 | async-start | bytes 2359296 | tf_op jit(solution)/shard_map/reduce_scatter | solution.py:54
  262.1 9.4 %copy-start.3 = (s32[128]{0:T(128)S(1)}, s32[128]{0:T(128)}, u32[]{:S(2)}) copy-start(s32[128]{0:T(128)} %param.13) | copy-start | bytes 1540
  283.8 93.2 %reduce-scatter.5.cloned.1.call-start = ((), (), s32[]{:S(2)}) async-start(), calls=%async_computation.5 | async-start | bytes 2359296 | tf_op jit(solution)/shard_map/reduce_scatter | solution.py:54
  322.7 54.4 %copy-start = (f32[512,128]{1,0:T(8,128)S(1)}, f32[512,128]{1,0:T(8,128)}, u32[]{:S(2)}) copy-start(f32[512,128]{1,0:T(8,128)} %param.8) | copy-start | bytes 786436
  335.1 84.1 %all-gather.11.cloned.1.call-start = ((), (), s32[]{:S(2)}) async-start(), calls=%async_computation.10 | async-start | bytes 2359296 | tf_op jit(solution)/shard_map/all_gather | solution.py:57
  379.1 171.6 %reduce-scatter.11.cloned.1.call-start = ((), (), s32[]{:S(2)}) async-start(), calls=%async_computation.11 | async-start | bytes 2162688 | tf_op jit(solution)/shard_map/reduce_scatter | solution.py:59
  453.5 97.1 %copy-start.2 = (f32[128,128]{1,0:T(8,128)S(1)}, f32[128,128]{1,0:T(8,128)}, u32[]{:S(2)}) copy-start(f32[128,128]{1,0:T(8,128)} %reduce-scatter.7.cloned.1.call-done) | copy-start | bytes 196612
Sparse Core Ops, SparseCore 0:
  10.4 44.0 all-gather.6
  101.2 84.6 reduce-scatter.6
  189.0 48.1 all-gather.8
  240.2 48.1 all-gather.4
  290.8 41.5 reduce-scatter.8
  335.2 41.8 reduce-scatter.4
  379.2 39.9 all-gather.10
  465.9 84.6 reduce-scatter.10
where the time goes:
time: 569 us; the launch traced here: 559 us
  waiting for transfers between devices  348 us (61%)
  matrix products  119 us (21%)
  local copies, waits for them, and re-layouts  67.5 us (12%)
  between operations  15.1 us (3%)
  other arithmetic  8.25 us (1%)
    reduce_scatter x2, waiting for transfers between devices, per_device(): lax.psum_scatter(partial_items, 'au', scatter_dimension=0, tiled=True)  170 us
    all_gather x2, waiting for transfers between devices, per_device(): lax.all_gather(items_now * norm_item, 'au', axis=0, tiled=True)  52.9 us
    all_gather x1, waiting for transfers between devices, per_device(): lax.all_gather(user_emb * norm_user, 'ia', axis=0, tiled=True)  43.4 us
    reduce_scatter x2, waiting for transfers between devices, per_device(): lax.psum_scatter(partial_users, 'ia', scatter_dimension=0, tiled=True)  41.9 us
    all_gather x1, waiting for transfers between devices, per_device(): lax.all_gather(users_now * norm_user, 'ia', axis=0, tiled=True)  39.8 us
    dot_general x2, matrix products, per_device(): jnp.einsum('tuk,tud->tkd', tiles, picked, precision=lax.Precision.HIGHEST)  38 us
    dot_general x2, matrix products, per_device(): jnp.einsum('tuk,tkd->tud', tiles, toward_picked, precision=lax.Precision....  38 us
    dot_general x2, matrix products, per_device(): jnp.dot(user_pick, toward_products.reshape(tile_count, -1), precision=lax...  21.5 us
  transfers between devices with their start and end apart: 8, of which 7 were waited for; matrix products, arithmetic and copies ran while one was open for 17% of the time, Pallas kernels for 0%

commit v1 on v0

--- a/solution.py
+++ b/solution.py
@@ -31,7 +31,9 @@
     ).astype(jnp.float32) * live_mask[None, :]
     norm_user = lax.rsqrt(user_degree.astype(jnp.float32))[:, None]
     norm_item = lax.rsqrt(item_degree.astype(jnp.float32))[:, None]
-    gathered_users = lax.all_gather(user_emb * norm_user, "ia", axis=0, tiled=True)
+    gathered_users = jnp.concatenate(
+        lax.all_to_all(jnp.stack([user_emb * norm_user] * lax.axis_size("ia")), "ia", 0, 0), axis=0
+    )
     users_now, items_now = (user_emb, item_emb)
     user_total, item_total = (user_emb, item_emb)
     for layer_index in range(LAYERS):

time: 569 us -> 581 us (1.021)
  starting transfers between devices: 1.18 us -> 9.6 us
    all_to_all x0 -> x1, waiting for transfers between devices: none -> 49.8 us  [per_device(): lax.all_to_all(jnp.stack([user_emb * norm_user] * lax.axis_size('ia')), '...]
    all_gather x1 -> x0, waiting for transfers between devices: 43.4 us -> none  [per_device(): lax.all_gather(user_emb * norm_user, 'ia', axis=0, tiled=True)]
    all_to_all x0 -> x1, starting transfers between devices: none -> 8.47 us  [per_device(): lax.all_to_all(jnp.stack([user_emb * norm_user] * lax.axis_size('ia')), '...]
  transfers between devices with their start and end apart: 8 -> 8, of which waited for: 7 -> 7; matrix products, arithmetic and copies ran while one was open for 17% -> 16% of each run, Pallas kernels for 0% -> 0%
where the time goes in v1:
time: 581 us; the launch traced here: 571 us
  waiting for transfers between devices  353 us (61%)
  matrix products  119 us (20%)
  local copies, waits for them, and re-layouts  67.2 us (12%)
  between operations  15.3 us (3%)
  starting transfers between devices  9.6 us (2%)
  other arithmetic  7.54 us (1%)
    reduce_scatter x2, waiting for transfers between devices, per_device(): lax.psum_scatter(partial_items, 'au', scatter_dimension=0, tiled=True)  167 us
    all_gather x2, waiting for transfers between devices, per_device(): lax.all_gather(items_now * norm_item, 'au', axis=0, tiled=True)  52.9 us
    all_to_all x1, waiting for transfers between devices, per_device(): lax.all_to_all(jnp.stack([user_emb * norm_user] * lax.axis_size('ia')), '...  49.8 us
    reduce_scatter x2, waiting for transfers between devices, per_device(): lax.psum_scatter(partial_users, 'ia', scatter_dimension=0, tiled=True)  42 us
    all_gather x1, waiting for transfers between devices, per_device(): lax.all_gather(users_now * norm_user, 'ia', axis=0, tiled=True)  39.8 us
    dot_general x2, matrix products, per_device(): jnp.einsum('tuk,tud->tkd', tiles, picked, precision=lax.Precision.HIGHEST)  38 us
    dot_general x2, matrix products, per_device(): jnp.einsum('tuk,tkd->tud', tiles, toward_picked, precision=lax.Precision....  38 us
    dot_general x2, matrix products, per_device(): jnp.dot(user_pick, toward_products.reshape(tile_count, -1), precision=lax...  21.5 us
  transfers between devices with their start and end apart: 8, of which 7 were waited for; matrix products, arithmetic and copies ran while one was open for 16% of the time, Pallas kernels for 0%

profile of v1, /device:TPU:2, one launch (start us, length us, event | category | flops | bytes accessed | tf_op | source)
XLA Modules:
  0.0 571.3 jit_solution(5379299357950344501)
XLA Ops:
  7.2 0.7 convert_rsqrt_fusion
  7.8 1.1 broadcast_multiply_fusion
  8.9 1.5 stack.2
  10.4 8.5 %all-to-all-start = ((f32[8,512,128]{2,1,0:T(8,128)}), f32[8,512,128]{2,1,0:T(8,128)S(1)}, u32[]{:S(2)}, u32[]{:S(2)}) async-start(f32[8,512,128]{2,1,0:T(8,128)} %stack.2), calls=%async_computation.1 | async-start | bytes 4194304 | tf_op jit(solution)/shard_map/all_to_all | solution.py:35
  18.9 0.0 reduce-scatter.7.cloned.1.call-start
  19.6 0.7 compare_select_fusion
  20.3 49.8 %all-to-all-done = f32[8,512,128]{2,1,0:T(8,128)S(1)} async-done(((f32[8,512,128]{2,1,0:T(8,128)}), f32[8,512,128]{2,1,0:T(8,128)S(1)}, u32[]{:S(2)}, u32[]{:S(2)}) %all-to-all-start) | async-done | bytes 2097184 | tf_op jit(solution)/shard_map/all_to_all | solution.py:35
  70.1 4.3 gather_fusion.1
  74.4 19.1 %convolution_bitcast_fusion.2 = f32[128,128,128]{1,2,0:T(8,128)} fusion(f32[128,128,128]{2,1,0:T(8,128)} %gather_fusion.1, f32[128,128,128]{2,1,0:T(8,128)} %param.12), kind=kOutput, calls=%fused_computation.6 | convolution fusion | flops 3221225472 | bytes 25165824 | tf_op jit(solution)/shard_map/tuk,tud->tkd/dot_general | solution.py:50
  93.5 9.4 %copy.13 = f32[128,128,128]{0,2,1:T(8,128)} copy(f32[128,128,128]{1,2,0:T(8,128)} %convolution_bitcast_fusion.2) | data formatting | bytes 16777216 | tf_op jit(solution)/shard_map/tuk,tud->tkd/dot_general | solution.py:50
  102.8 10.8 %fusion.2 = f32[32,16384]{1,0:T(8,128)S(1)} fusion(f32[128,16384]{0,1:T(8,128)} %bitcast.35, s32[128]{0:T(128)S(1)} %copy-done.4, f32[128]{0:T(128)S(1)} %compare_convert_fusion), kind=kOutput, calls=%fused_computation.16 | convolution fusion | flops 805314560 | bytes 10486784 | tf_op jit(solution)/shard_map/dot_general | solution.py:51
  113.6 1.5 reshape.52
  115.1 0.0 all-gather.6.cloned.1.call-start
  115.2 82.5 %reduce-scatter.7.cloned.1.call-done = f32[128,128]{1,0:T(8,128)} async-done(((f32[4096,128]{1,0:T(8,128)}), f32[128,128]{1,0:T(8,128)}) %reduce-scatter.7.cloned.1.call-update) | async-done | bytes 65552 | tf_op jit(solution)/shard_map/reduce_scatter | solution.py:61
  197.7 1.6 broadcast_multiply_fusion.1
  199.3 0.0 all-gather.6.cloned.1.call-update
  199.3 0.0 all-gather.4.cloned.1.call-start
  199.4 0.7 all-gather.4.cloned.1.call-update
  200.1 0.5 reduce-scatter.9.cloned.1.call-start
  200.6 48.4 %all-gather.6.cloned.1.call-done = f32[4096,128]{1,0:T(8,128)} async-done(((f32[128,128]{1,0:T(8,128)}), f32[4096,128]{1,0:T(8,128)}) %all-gather.6.cloned.1.call-update) | async-done | bytes 2097168 | tf_op jit(solution)/shard_map/all_gather | solution.py:40
  249.0 5.9 %gather_fusion.2 = f32[128,128,128]{2,1,0:T(8,128)} fusion(f32[32,128,128]{2,1,0:T(8,128)} %bitcast.32, s32[1024]{0:T(1024)S(1)} %pad_clamp_fusion.1), kind=kCustom, calls=%fused_computation.2 | custom fusion | bytes 16777728 | tf_op jit(solution)/shard_map/gather | solution.py:41
  255.0 19.0 %convolution_bitcast_fusion.1 = f32[128,128,128]{1,2,0:T(8,128)} fusion(f32[128,128,128]{2,1,0:T(8,128)} %gather_fusion.2, f32[128,128,128]{2,1,0:T(8,128)} %param.12), kind=kOutput, calls=%fused_computation.5 | convolution fusion | flops 3221225472 | bytes 25165824 | tf_op jit(solution)/shard_map/tuk,tkd->tud/dot_general | solution.py:42
  273.9 9.4 %copy.15 = f32[128,128,128]{0,2,1:T(8,128)} copy(f32[128,128,128]{1,2,0:T(8,128)} %convolution_bitcast_fusion.1) | data formatting | bytes 16777216 | tf_op jit(solution)/shard_map/tuk,tkd->tud/dot_general | solution.py:42
  283.4 10.7 %fusion.4 = f32[32,16384]{1,0:T(8,128)S(1)} fusion(f32[128,16384]{0,1:T(8,128)} %bitcast.36, f32[128]{0:T(128)S(1)} %compare_convert_fusion, s32[128]{0:T(128)S(1)} %copy-done.3), kind=kOutput, calls=%fused_computation.18 | convolution fusion | flops 805314560 | bytes 10486784 | tf_op jit(solution)/shard_map/dot_general | solution.py:45
  294.1 1.5 reshape.55
  295.6 0.0 reduce-scatter.9.cloned.1.call-update
  295.6 0.2 reduce-scatter.5.cloned.1.call-start
  295.8 4.5 all-gather.4.cloned.1.call-done
  300.3 5.9 %gather_fusion = f32[128,128,128]{2,1,0:T(8,128)} fusion(f32[32,128,128]{2,1,0:T(8,128)} %bitcast.31, s32[1024]{0:T(1024)S(1)} %pad_clamp_fusion.1), kind=kCustom, calls=%fused_computation | custom fusion | bytes 16777728 | tf_op jit(solution)/shard_map/gather | solution.py:41
  306.3 19.0 %convolution_bitcast_fusion.3 = f32[128,128,128]{1,2,0:T(8,128)} fusion(f32[128,128,128]{2,1,0:T(8,128)} %gather_fusion, f32[128,128,128]{2,1,0:T(8,128)} %param.12), kind=kOutput, calls=%fused_computation.7 | convolution fusion | flops 3221225472 | bytes 25165824 | tf_op jit(solution)/shard_map/tuk,tkd->tud/dot_general | solution.py:42
  325.2 9.4 %copy.11 = f32[128,128,128]{0,2,1:T(8,128)} copy(f32[128,128,128]{1,2,0:T(8,128)} %convolution_bitcast_fusion.3) | data formatting | bytes 16777216 | tf_op jit(solution)/shard_map/tuk,tkd->tud/dot_general | solution.py:42
  334.7 10.8 %fusion.6 = f32[32,16384]{1,0:T(8,128)S(1)} fusion(f32[128,16384]{0,1:T(8,128)} %bitcast.37, f32[128]{0:T(128)S(1)} %compare_convert_fusion, s32[128]{0:T(128)S(1)} %copy-done.3), kind=kOutput, calls=%fused_computation.20 | convolution fusion | flops 805314560 | bytes 10486784 | tf_op jit(solution)/shard_map/dot_general | solution.py:45
  345.5 1.5 reshape.50
  347.0 0.0 reduce-scatter.5.cloned.1.call-update
  347.0 0.0 all-gather.8.cloned.1.call-start
  347.1 0.0 reduce-scatter.9.cloned.1.call-done
  347.1 42.0 %reduce-scatter.5.cloned.1.call-done = f32[512,128]{1,0:T(8,128)} async-done(((f32[4096,128]{1,0:T(8,128)}), f32[512,128]{1,0:T(8,128)}) %reduce-scatter.5.cloned.1.call-update) | async-done | bytes 262160 | tf_op jit(solution)/shard_map/reduce_scatter | solution.py:56
  389.1 2.0 multiply_multiply_fusion
  391.0 0.0 all-gather.8.cloned.1.call-update
  391.1 0.3 reduce-scatter.11.cloned.1.call-start
  391.3 39.8 %all-gather.8.cloned.1.call-done = f32[4096,128]{1,0:T(8,128)} async-done(((f32[512,128]{1,0:T(8,128)}), f32[4096,128]{1,0:T(8,128)}) %all-gather.8.cloned.1.call-update) | async-done | bytes 2097168 | tf_op jit(solution)/shard_map/all_gather | solution.py:59
  431.1 5.9 %gather_fusion.3 = f32[128,128,128]{2,1,0:T(8,128)} fusion(f32[32,128,128]{2,1,0:T(8,128)} %bitcast.33, s32[1024]{0:T(1024)S(1)} %pad_clamp_fusion), kind=kCustom, calls=%fused_computation.3 | custom fusion | bytes 16777728 | tf_op jit(solution)/shard_map/gather | solution.py:49
  437.0 19.0 %convolution_bitcast_fusion = f32[128,128,128]{1,2,0:T(8,128)} fusion(f32[128,128,128]{2,1,0:T(8,128)} %gather_fusion.3, f32[128,128,128]{2,1,0:T(8,128)} %param.12), kind=kOutput, calls=%fused_computation.4 | convolution fusion | flops 3221225472 | bytes 25165824 | tf_op jit(solution)/shard_map/tuk,tud->tkd/dot_general | solution.py:50
  456.0 9.4 %copy.17 = f32[128,128,128]{0,2,1:T(8,128)} copy(f32[128,128,128]{1,2,0:T(8,128)} %convolution_bitcast_fusion) | data formatting | bytes 16777216 | tf_op jit(solution)/shard_map/tuk,tud->tkd/dot_general | solution.py:50
  465.4 10.7 %fusion = f32[32,16384]{1,0:T(8,128)S(1)} fusion(f32[128,16384]{0,1:T(8,128)} %bitcast.34, s32[128]{0:T(128)S(1)} %copy-done.4, f32[128]{0:T(128)S(1)} %compare_convert_fusion), kind=kOutput, calls=%fused_computation.14 | convolution fusion | flops 805314560 | bytes 10486784 | tf_op jit(solution)/shard_map/dot_general | solution.py:51
  476.2 1.5 reshape.58
  477.7 84.8 %reduce-scatter.11.cloned.1.call-done = f32[128,128]{1,0:T(8,128)} async-done(((f32[4096,128]{1,0:T(8,128)}), f32[128,128]{1,0:T(8,128)}) %reduce-scatter.11.cloned.1.call-update) | async-done | bytes 65552 | tf_op jit(solution)/shard_map/reduce_scatter | solution.py:61
  562.5 1.6 add_multiply_fusion.1
  (19 shorter events, 0.1 us)
Async XLA Ops:
  10.4 59.7 %all-to-all-start = ((f32[8,512,128]{2,1,0:T(8,128)}), f32[8,512,128]{2,1,0:T(8,128)S(1)}, u32[]{:S(2)}, u32[]{:S(2)}) async-start(f32[8,512,128]{2,1,0:T(8,128)} %stack.2), calls=%async_computation.1 | async-start | bytes 4194304 | tf_op jit(solution)/shard_map/all_to_all | solution.py:35
  18.9 178.9 %reduce-scatter.7.cloned.1.call-start = ((), (), s32[]{:S(2)}) async-start(), calls=%async_computation.7 | async-start | bytes 2162688 | tf_op jit(solution)/shard_map/reduce_scatter | solution.py:61
  93.5 9.4 %copy-start.4 = (s32[128]{0:T(128)S(1)}, s32[128]{0:T(128)}, u32[]{:S(2)}) copy-start(s32[128]{0:T(128)} %param.14) | copy-start | bytes 1540
  102.8 12.4 %copy-start.5 = (s32[128]{0:T(128)S(1)}, s32[128]{0:T(128)}, u32[]{:S(2)}) copy-start(s32[128]{0:T(128)} %param.11) | copy-start | bytes 1540
  102.8 94.9 %copy-start.1 = (f32[128,128]{1,0:T(8,128)S(1)}, f32[128,128]{1,0:T(8,128)}, u32[]{:S(2)}) copy-start(f32[128,128]{1,0:T(8,128)} %param.9) | copy-start | bytes 196612
  115.1 133.9 %all-gather.6.cloned.1.call-start = ((), (), s32[]{:S(2)}) async-start(), calls=%async_computation.8 | async-start | bytes 2162688 | tf_op jit(solution)/shard_map/all_gather | solution.py:40
  199.3 101.0 %all-gather.4.cloned.1.call-start = ((), (), s32[]{:S(2)}) async-start(), calls=%async_computation.5 | async-start | bytes 2162688 | tf_op jit(solution)/shard_map/all_gather | solution.py:40
  200.1 147.0 %reduce-scatter.9.cloned.1.call-start = ((), (), s32[]{:S(2)}) async-start(), calls=%async_computation.9 | async-start | bytes 2359296 | tf_op jit(solution)/shard_map/reduce_scatter | solution.py:56
  273.9 9.4 %copy-start.3 = (s32[128]{0:T(128)S(1)}, s32[128]{0:T(128)}, u32[]{:S(2)}) copy-start(s32[128]{0:T(128)} %param.13) | copy-start | bytes 1540
  295.6 93.5 %reduce-scatter.5.cloned.1.call-start = ((), (), s32[]{:S(2)}) async-start(), calls=%async_computation.6 | async-start | bytes 2359296 | tf_op jit(solution)/shard_map/reduce_scatter | solution.py:56
  334.7 54.4 %copy-start = (f32[512,128]{1,0:T(8,128)S(1)}, f32[512,128]{1,0:T(8,128)}, u32[]{:S(2)}) copy-start(f32[512,128]{1,0:T(8,128)} %param.8) | copy-start | bytes 786436
  347.0 84.1 %all-gather.8.cloned.1.call-start = ((), (), s32[]{:S(2)}) async-start(), calls=%async_computation.10 | async-start | bytes 2359296 | tf_op jit(solution)/shard_map/all_gather | solution.py:59
  391.1 171.5 %reduce-scatter.11.cloned.1.call-start = ((), (), s32[]{:S(2)}) async-start(), calls=%async_computation.11 | async-start | bytes 2162688 | tf_op jit(solution)/shard_map/reduce_scatter | solution.py:61
  465.4 97.1 %copy-start.2 = (f32[128,128]{1,0:T(8,128)S(1)}, f32[128,128]{1,0:T(8,128)}, u32[]{:S(2)}) copy-start(f32[128,128]{1,0:T(8,128)} %reduce-scatter.7.cloned.1.call-done) | copy-start | bytes 196612
Sparse Core Ops, SparseCore 0:
  115.3 82.4 reduce-scatter.6
  200.9 48.1 all-gather.5
  252.2 48.1 all-gather.3
  302.7 41.5 reduce-scatter.8
  347.1 41.8 reduce-scatter.4
  391.2 39.8 all-gather.7
  477.8 84.6 reduce-scatter.10
